TPU v7x, 128 devices: a whole 4x4x4 slice. The times are simulated.
128 devices in a mesh: tx: 8 (over z_hi, y), ty: 16 (over x, z_lo, core).
Axes of the slice: x: 4, y: 4, z: 4 (z_hi: 2, z_lo: 2; z = z_hi * 2 + z_lo), core: 2. Of those that a mesh axis runs over, the one named last changes fastest.
Arguments:
- states: bfloat16 [2, 256, 16384], P(None, 'ty', 'tx')
- norm_gain: bfloat16 [16384], P('tx'), may hold values from 0.099609375 to 1.8984375
- w_gate: bfloat16 [16384, 26624], P('tx', 'ty'), may hold values from -0.046875 to 0.046875
- w_up: bfloat16 [16384, 26624], P('tx', 'ty'), may hold values from -0.046875 to 0.046875
- w_down: bfloat16 [26624, 16384], P('ty', 'tx'), may hold values from -0.0390625 to 0.0390625
- w_qkv: bfloat16 [16384, 3, 4096], P('tx', None, 'ty'), may hold values from -0.046875 to 0.046875
- w_class: bfloat16 [4096, 14], P('ty'), may hold values from -0.375 to 0.375
- cache_keys: bfloat16 [256, 64, 4096], P('tx', None, 'ty')
- cache_values: bfloat16 [256, 64, 4096], P('tx', None, 'ty'), may hold values from -6 to 6
- cache_lengths: int32 [256], P('tx'), may hold values from 1 to 64, as said below
- row_slots: int32 [256], replicated, may hold values from 0 to 255, each once
Outputs:
- stream_out: bfloat16 [2, 256, 16384], P(None, 'ty', 'tx')
- category_logits: float32 [2, 256, 14], replicated
Inputs may be any that keep to these rules, and one draw needn't show every extreme that they name: `cache_lengths`: some slot has exactly 64 live positions. `row_slots`: each cache slot belongs to exactly one row.
All inputs are finite; a program needn't handle non-finite values.
Results may differ from a plain program's by a relative error of at most 0.015.
The roundings to bfloat16 on the way count: a program that leaves them out, or rounds other values in their place, can miss the bound.
Values may be sent and summed in bfloat16 or wider, within the bound.
No kernel may reach another device: no remote copies, remote signals or barrier semaphores. Data moves between devices by JAX's collectives and lax.ppermute only.
A program may use at most 128 MiB of HBM per device.

v0:
```python
import jax
import jax.numpy as jnp
from jax import lax
from jax.sharding import PartitionSpec as P

D = 16384
HEAD_DIM = 128


def per_device(
    states,
    norm_gain,
    w_gate,
    w_up,
    w_down,
    w_qkv,
    w_class,
    cache_keys,
    cache_values,
    cache_lengths,
    row_slots,
):
    steps_count = states.shape[0]
    local_rows = states.shape[1]
    total_rows = row_slots.shape[0]
    owner_rows = cache_keys.shape[0]
    history = cache_keys.shape[1]
    local_width = w_qkv.shape[2]
    heads_here = local_width // HEAD_DIM
    values_f = states.astype(jnp.float32)
    squares = lax.psum(jnp.sum(values_f * values_f, axis=2), "tx")
    scale = lax.rsqrt(squares / D + 1e-05)
    normed_local = (values_f * scale[:, :, None] * norm_gain.astype(jnp.float32)).astype(
        jnp.bfloat16
    )
    normed = lax.all_gather(normed_local, "ty", axis=1, tiled=True)
    slot_rows = (
        jnp.zeros((total_rows,), jnp.int32)
        .at[row_slots]
        .set(jnp.arange(total_rows, dtype=jnp.int32))
    )
    qkv_weight = w_qkv.reshape(w_qkv.shape[0], 3 * local_width)
    outputs = []
    partials = []
    new_keys = []
    new_values = []
    for step in range(steps_count):
        normed_step = normed[step]
        gate, up = lax.psum(
            (
                jnp.dot(normed_step, w_gate, preferred_element_type=jnp.float32),
                jnp.dot(normed_step, w_up, preferred_element_type=jnp.float32),
            ),
            "tx",
        )
        hidden = (jax.nn.silu(gate) * up).astype(jnp.bfloat16)

        def down_term(start, count, source=hidden):
            return jnp.dot(source, w_down, preferred_element_type=jnp.float32)

        mixed = lax.psum_scatter(
            down_term(jnp.int32(0), local_rows * lax.axis_size("ty")),
            "ty",
            scatter_dimension=0,
            tiled=True,
        )
        stream = (values_f[step] + mixed).astype(jnp.bfloat16)
        outputs.append(stream)
        stream_all = lax.all_gather(stream, "ty", axis=0, tiled=True)
        ordered = jnp.take(stream_all, slot_rows, axis=0)
        full = lax.psum(jnp.dot(ordered, qkv_weight, preferred_element_type=jnp.float32), "tx")
        owned = lax.dynamic_slice_in_dim(full, lax.axis_index("tx") * owner_rows, owner_rows, 0)
        triple = owned.astype(jnp.bfloat16).reshape(owner_rows, 3, local_width)
        query = triple[:, 0]
        new_keys.append(triple[:, 1])
        new_values.append(triple[:, 2])
        keys = jnp.concatenate([cache_keys, jnp.stack(new_keys, axis=1)], axis=1)
        vals = jnp.concatenate([cache_values, jnp.stack(new_values, axis=1)], axis=1)
        count_keys = keys.shape[1]
        query_h = query.reshape(owner_rows, heads_here, HEAD_DIM)
        keys_h = keys.reshape(owner_rows, count_keys, heads_here, HEAD_DIM)
        vals_h = vals.reshape(owner_rows, count_keys, heads_here, HEAD_DIM)
        scores = jnp.einsum(
            "shd,slhd->shl", query_h, keys_h, preferred_element_type=jnp.float32
        ) * HEAD_DIM ** (-0.5)
        where_pos = jnp.arange(count_keys, dtype=jnp.int32)
        valid = (where_pos[None, :] < cache_lengths[:, None]) | (where_pos[None, :] >= history)
        scores = jnp.where(valid[:, None, :], scores, jnp.float32(-1e30))
        top = jnp.max(scores, axis=2, keepdims=True)
        expo = jnp.exp(scores - top)
        weights = (expo / jnp.sum(expo, axis=2, keepdims=True)).astype(jnp.bfloat16)
        attended = jnp.einsum("shl,slhd->shd", weights, vals_h, preferred_element_type=jnp.float32)
        attended = attended.reshape(owner_rows, local_width).astype(jnp.bfloat16)
        partials.append(jnp.dot(attended, w_class, preferred_element_type=jnp.float32))
    stacked = jnp.stack(partials, axis=0)
    summed = lax.psum(stacked, "ty")
    by_slot = lax.all_gather(summed, "tx", axis=1, tiled=True)
    category_logits = jnp.take(by_slot, row_slots, axis=1)
    return (jnp.stack(outputs, axis=0), category_logits)


def solution(mesh):
    return jax.shard_map(
        per_device,
        mesh=mesh,
        in_specs=(
            P(None, "ty", "tx"),
            P("tx"),
            P("tx", "ty"),
            P("tx", "ty"),
            P("ty", "tx"),
            P("tx", None, "ty"),
            P("ty", None),
            P("tx", None, "ty"),
            P("tx", None, "ty"),
            P("tx"),
            P(),
        ),
        out_specs=(P(None, "ty", "tx"), P()),
        check_vma=False,
    )
```

profile of v0, /device:TPU:0, one launch (start us, length us, event | category | flops | bytes accessed | tf_op | source)
XLA Modules:
  0.0 643.5 jit_solution(3496387815426926068)
XLA Ops:
  8.9 25.4 %psum.56 = f32[2,16]{1,0:T(2,128)S(1)} all-reduce(f32[2,16]{1,0:T(2,128)S(1)} %multiply_reduce_fusion), channel_id=1, replica_groups=mesh['tx'=8,'ty'=16] {'tx'}, use_global_device_ids=true, to_apply=%region_1.0 | all-reduce | flops 32 | bytes 256 | tf_op jit(solution)/shard_map/psum | solution.py:31
  36.0 30.8 %all-gather.4.cloned.1.call-done = bf16[2,256,2048]{2,1,0:T(8,128)(2,1)} async-done(((bf16[2,16,2048]{2,1,0:T(8,128)(2,1)}), bf16[2,256,2048]{2,1,0:T(8,128)(2,1)}) %all-gather.4.cloned.1.call-update) | async-done | bytes 2097168 | tf_op jit(solution)/shard_map/all_gather | solution.py:36
  66.9 6.7 %fusion.28 = f32[256,1664]{1,0:T(8,128)} fusion(bf16[2048,1664]{1,0:T(8,128)(2,1)} %param.16, bf16[2,256,2048]{2,1,0:T(8,128)(2,1)} %all-gather.4.cloned.1.call-done), kind=kOutput, calls=%fused_computation.42 | convolution fusion | flops 1744830464 | bytes 9568256 | tf_op jit(solution)/shard_map/dot_general | solution.py:52
  73.6 6.4 fusion.30
  80.0 3.3 fusion.29
  83.3 3.3 fusion.31
  86.6 157.6 %all-reduce.5.cloned.1.call-done = (f32[256,1664]{1,0:T(8,128)}, f32[256,1664]{1,0:T(8,128)}, f32[256,1664]{1,0:T(8,128)}, f32[256,1664]{1,0:T(8,128)}) async-done(((f32[256,1664]{1,0:T(8,128)}, f32[256,1664]{1,0:T(8,128)}, f32[256,1664]{1,0:T(8,128)}, f32[256,1664]{1,0:T(8,128)}), (f32[256,1664]{1,0:T(8,128)}, f32[256,1664]{1,0:T(8,128)}, f32[256,1664]{1,0:T(8,128)}, ...) | async-done | bytes 6815760 | tf_op jit(solution)/shard_map/psum | solution.py:49
  244.2 7.5 %fusion.33 = f32[256,2048]{1,0:T(8,128)} fusion(bf16[1664,2048]{1,0:T(8,128)(2,1)} %param.17, f32[256,1664]{1,0:T(8,128)} %get-tuple-element.13, f32[256,1664]{1,0:T(8,128)} %get-tuple-element.14), kind=kOutput, calls=%fused_computation.47 | convolution fusion | flops 1747386368 | bytes 12320768 | tf_op jit(solution)/shard_map/dot_general | solution.py:59
  253.1 7.0 %fusion.32 = f32[256,2048]{1,0:T(8,128)} fusion(bf16[1664,2048]{1,0:T(8,128)(2,1)} %param.17, f32[256,1664]{1,0:T(8,128)S(1)} %copy-done.11, f32[256,1664]{1,0:T(8,128)} %get-tuple-element.16), kind=kOutput, calls=%fused_computation.46 | convolution fusion | flops 1747386368 | bytes 12320768 | tf_op jit(solution)/shard_map/dot_general | solution.py:59
  260.3 53.0 %reduce-scatter.5.cloned.1.call-done = f32[16,2048]{1,0:T(8,128)} async-done(((f32[256,2048]{1,0:T(8,128)}), f32[16,2048]{1,0:T(8,128)}) %reduce-scatter.5.cloned.1.call-update) | async-done | bytes 131088 | tf_op jit(solution)/shard_map/reduce_scatter | solution.py:61
  313.3 64.4 %reduce-scatter.3.cloned.1.call-done = f32[16,2048]{1,0:T(8,128)} async-done(((f32[256,2048]{1,0:T(8,128)}), f32[16,2048]{1,0:T(8,128)}) %reduce-scatter.3.cloned.1.call-update) | async-done | bytes 131088 | tf_op jit(solution)/shard_map/reduce_scatter | solution.py:61
  377.7 1.7 fusion.41
  380.1 3.1 copy.28
  385.5 24.7 %all-gather.8.cloned.1.call-done = bf16[256,2048]{1,0:T(8,128)(2,1)} async-done(((bf16[16,2048]{1,0:T(8,128)(2,1)}), bf16[256,2048]{1,0:T(8,128)(2,1)}) %all-gather.8.cloned.1.call-update) | async-done | bytes 1048592 | tf_op jit(solution)/shard_map/all_gather | solution.py:69
  410.2 4.7 gather_fusion.2
  415.0 3.2 fusion.22
  418.2 26.1 %all-gather.6.cloned.1.call-done = bf16[256,2048]{1,0:T(8,128)(2,1)} async-done(((bf16[16,2048]{1,0:T(8,128)(2,1)}), bf16[256,2048]{1,0:T(8,128)(2,1)}) %all-gather.6.cloned.1.call-update) | async-done | bytes 1048592 | tf_op jit(solution)/shard_map/all_gather | solution.py:69
  444.3 4.7 gather_fusion.1
  449.0 3.2 fusion.24
  452.2 83.2 %all-reduce.6 = (bf16[256,768]{1,0:T(8,128)(2,1)S(1)}, bf16[256,768]{1,0:T(8,128)(2,1)S(1)}) all-reduce(f32[256,768]{1,0:T(8,128)} %fusion.22, f32[256,768]{1,0:T(8,128)} %fusion.24), channel_id=1, replica_groups=mesh['tx'=8,'ty'=16] {'tx'}, use_global_device_ids=true, to_apply=%region_12.14 | all-reduce | flops 393216 | bytes 2359296 | tf_op jit(solution)/shard_map/psum | solution.py:71
  537.0 1.9 fusion.10
  543.8 1.9 fusion.6
  547.2 52.9 %psum.63 = f32[2,32,14]{1,2,0:T(8,128)S(1)} all-reduce(f32[2,32,14]{1,2,0:T(8,128)S(1)} %pad_maximum_fusion.5), channel_id=1, replica_groups=mesh['tx'=8,'ty'=16] {'ty'}, use_global_device_ids=true, to_apply=%region_15.17 | all-reduce | flops 896 | bytes 7168 | tf_op jit(solution)/shard_map/psum | solution.py:96
  600.2 34.4 %all_gather.15 = f32[2,256,14]{2,0,1:T(2,128)S(1)} all-gather(f32[2,32,14]{2,0,1:T(2,128)S(1)} %copy.33), channel_id=1, replica_groups=mesh['tx'=8,'ty'=16] {'tx'}, dimensions={1}, use_global_device_ids=true | all-gather | bytes 32256 | tf_op jit(solution)/shard_map/all_gather | solution.py:97
  (85 shorter events, 17.9 us)
Async XLA Ops:
  7.2 539.8 %copy-start = (bf16[256,14]{0,1:T(8,128)(2,1)S(1)}, bf16[256,14]{0,1:T(8,128)(2,1)}, u32[]{:S(2)}) copy-start(bf16[256,14]{0,1:T(8,128)(2,1)} %param.19) | copy-start | bytes 21508
  7.2 59.7 %all-gather.4.cloned.1.call-start = ((), (), s32[]{:S(2)}) async-start(), calls=%async_computation.2 | async-start | bytes 2228224 | tf_op jit(solution)/shard_map/all_gather | solution.py:36
  36.0 208.2 %all-reduce.5.cloned.1.call-start = ((), (), s32[]{:S(2)}) async-start(), calls=%async_computation.7 | async-start | bytes 13631488 | tf_op jit(solution)/shard_map/psum | solution.py:49
  66.9 6.7 %copy-start.10 = (bf16[2,256,2048]{2,1,0:T(8,128)(2,1)S(1)}, bf16[2,256,2048]{2,1,0:T(8,128)(2,1)}, u32[]{:S(2)}) copy-start(bf16[2,256,2048]{2,1,0:T(8,128)(2,1)} %all-gather.4.cloned.1.call-done) | copy-start | bytes 6291460
  66.9 13.1 %slice-start = ((s8[6815744]{0:T(1024)(128)(4,1)}), s8[4194304]{0:T(1024)(128)(4,1)S(1)}, s32[]{:S(2)}) async-start(s8[6815744]{0:T(1024)(128)(4,1)} %bitcast.87), calls=%async_computation.8 | async-start | bytes 8388608
  73.6 6.4 slice-start.1
  86.6 226.7 %reduce-scatter.5.cloned.1.call-start = ((), (), s32[]{:S(2)}) async-start(), calls=%async_computation.4 | async-start | bytes 2228224 | tf_op jit(solution)/shard_map/reduce_scatter | solution.py:61
  251.7 1.5 copy-start.11
  251.7 126.0 %reduce-scatter.3.cloned.1.call-start = ((), (), s32[]{:S(2)}) async-start(), calls=%async_computation.3 | async-start | bytes 2228224 | tf_op jit(solution)/shard_map/reduce_scatter | solution.py:61
  253.1 7.1 %copy-start.5 = (bf16[2,16,2048]{2,1,0:T(8,128)(2,1)S(1)}, bf16[2,16,2048]{2,1,0:T(8,128)(2,1)}, u32[]{:S(2)}) copy-start(bf16[2,16,2048]{2,1,0:T(8,128)(2,1)} %param.13) | copy-start | bytes 393220
  260.1 119.5 %copy-start.9 = (s32[256]{0:T(256)S(1)}, s32[256]{0:T(256)}, u32[]{:S(2)}) copy-start(s32[256]{0:T(256)} %param.23) | copy-start | bytes 3076
  260.1 119.9 %copy-start.3 = (bf16[2048,3,256]{2,0,1:T(8,128)(2,1)S(1)}, bf16[2048,3,256]{2,0,1:T(8,128)(2,1)}, u32[]{:S(2)}) copy-start(bf16[2048,3,256]{2,0,1:T(8,128)(2,1)} %param.18) | copy-start | bytes 9437188
  260.2 150.0 %all-gather.8.cloned.1.call-start = ((), (), s32[]{:S(2)}) async-start(), calls=%async_computation.6 | async-start | bytes 1114112 | tf_op jit(solution)/shard_map/all_gather | solution.py:69
  379.4 64.9 %all-gather.6.cloned.1.call-start = ((), (), s32[]{:S(2)}) async-start(), calls=%async_computation.5 | async-start | bytes 1114112 | tf_op jit(solution)/shard_map/all_gather | solution.py:69
  380.0 4.6 copy-start.8
  380.0 4.8 copy-start.6
  380.1 4.8 copy-start.7
  385.5 29.4 %copy-start.4 = (bf16[2048,3,256]{0,2,1:T(8,128)(2,1)S(1)}, bf16[2048,3,256]{0,2,1:T(8,128)(2,1)}, u32[]{:S(2)}) copy-start(bf16[2048,3,256]{0,2,1:T(8,128)(2,1)} %copy.28) | copy-start | bytes 9437188
  452.2 83.3 %copy-start.1 = (bf16[32,64,256]{2,1,0:T(8,128)(2,1)S(1)}, bf16[32,64,256]{2,1,0:T(8,128)(2,1)}, u32[]{:S(2)}) copy-start(bf16[32,64,256]{2,1,0:T(8,128)(2,1)} %param.20) | copy-start | bytes 3145732
  535.6 3.3 copy-start.2
Sparse Core Ops, SparseCore 0:
  36.1 30.7 all-gather.3
  86.7 157.4 all-reduce.4
  251.8 61.4 reduce-scatter.4
  315.5 62.1 reduce-scatter.2
  379.5 30.6 all-gather.7
  411.8 32.4 all-gather.5
where the time goes:
time: 644 us
  waiting for transfers between devices  357 us (55%)
  blocking collectives  196 us (30%)
  matrix products  46.8 us (7%)
  local copies, waits for them, and re-layouts  21.8 us (3%)
  between operations  14.4 us (2%)
  other arithmetic  7.17 us (1%)
    psum x1, waiting for transfers between devices, per_device(): lax.psum((jnp.dot(normed_step, w_gate, preferred_element_type=jnp.float32...  158 us
    reduce_scatter x2, waiting for transfers between devices, per_device(): lax.psum_scatter(down_term(jnp.int32(0), local_rows * lax.axis_size('ty')...  117 us
    psum x1, blocking collectives, per_device(): lax.psum(jnp.dot(ordered, qkv_weight, preferred_element_type=jnp.float32)...  83.2 us
    psum x1, blocking collectives, per_device(): summed = lax.psum(stacked, 'ty')  52.9 us
    all_gather x2, waiting for transfers between devices, per_device(): stream_all = lax.all_gather(stream, 'ty', axis=0, tiled=True)  50.8 us
    all_gather x1, blocking collectives, per_device(): by_slot = lax.all_gather(summed, 'tx', axis=1, tiled=True)  34.4 us
    all_gather x1, waiting for transfers between devices, per_device(): normed = lax.all_gather(normed_local, 'ty', axis=1, tiled=True)  30.8 us
    psum x1, blocking collectives, per_device(): squares = lax.psum(jnp.sum(values_f * values_f, axis=2), 'tx')  25.4 us
  transfers between devices with their start and end apart: 6, of which 6 were waited for; matrix products, arithmetic and copies ran while one was open for 3% of the time, Pallas kernels for 0%

commit v1 on v0

--- a/solution.py
+++ b/solution.py
@@ -68,7 +68,9 @@
         outputs.append(stream)
         stream_all = lax.all_gather(stream, "ty", axis=0, tiled=True)
         ordered = jnp.take(stream_all, slot_rows, axis=0)
-        full = lax.psum(jnp.dot(ordered, qkv_weight, preferred_element_type=jnp.float32), "tx")
+        xin = jnp.dot(ordered, qkv_weight, preferred_element_type=jnp.float32)
+        o_now = lax.all_gather(xin, axis_name="tx")
+        full = jnp.sum(o_now, axis=0)
         owned = lax.dynamic_slice_in_dim(full, lax.axis_index("tx") * owner_rows, owner_rows, 0)
         triple = owned.astype(jnp.bfloat16).reshape(owner_rows, 3, local_width)
         query = triple[:, 0]

time: 644 us -> 741 us (1.15)
  waiting for transfers between devices: 357 us -> 529 us
  blocking collectives: 196 us -> 114 us
    all_gather x0 -> x2, waiting for transfers between devices: none -> 170 us  [per_device(): o_now = lax.all_gather(xin, axis_name='tx')]
    psum x1 -> x0, blocking collectives: 83.2 us -> none  [per_device(): lax.psum(jnp.dot(ordered, qkv_weight, preferred_element_type=jnp.float32)...]
  transfers between devices with their start and end apart: 6 -> 8, of which waited for: 6 -> 8; matrix products, arithmetic and copies ran while one was open for 3% -> 4% of each run, Pallas kernels for 0% -> 0%
where the time goes in v1:
time: 741 us; the launch traced here: 740 us
  waiting for transfers between devices  529 us (71%)
  blocking collectives  114 us (15%)
  matrix products  46.6 us (6%)
  local copies, waits for them, and re-layouts  21.8 us (3%)
  between operations  14.4 us (2%)
  other arithmetic  13.6 us (2%)
    all_gather x2, waiting for transfers between devices, per_device(): o_now = lax.all_gather(xin, axis_name='tx')  170 us
    psum x1, waiting for transfers between devices, per_device(): lax.psum((jnp.dot(normed_step, w_gate, preferred_element_type=jnp.float32...  158 us
    reduce_scatter x2, waiting for transfers between devices, per_device(): lax.psum_scatter(down_term(jnp.int32(0), local_rows * lax.axis_size('ty')...  117 us
    psum x1, blocking collectives, per_device(): summed = lax.psum(stacked, 'ty')  54.6 us
    all_gather x2, waiting for transfers between devices, per_device(): stream_all = lax.all_gather(stream, 'ty', axis=0, tiled=True)  52.4 us
    all_gather x1, blocking collectives, per_device(): by_slot = lax.all_gather(summed, 'tx', axis=1, tiled=True)  34.4 us
    all_gather x1, waiting for transfers between devices, per_device(): normed = lax.all_gather(normed_local, 'ty', axis=1, tiled=True)  30.8 us
    psum x1, blocking collectives, per_device(): squares = lax.psum(jnp.sum(values_f * values_f, axis=2), 'tx')  25.4 us
  transfers between devices with their start and end apart: 8, of which 8 were waited for; matrix products, arithmetic and copies ran while one was open for 4% of the time, Pallas kernels for 0%

profile of v1, /device:TPU:0, one launch (start us, length us, event | category | flops | bytes accessed | tf_op | source)
XLA Modules:
  0.0 740.0 jit_solution(3649653066351289969)
XLA Ops:
  8.9 25.4 %psum.42 = f32[2,16]{1,0:T(2,128)S(1)} all-reduce(f32[2,16]{1,0:T(2,128)S(1)} %multiply_reduce_fusion), channel_id=1, replica_groups=mesh['tx'=8,'ty'=16] {'tx'}, use_global_device_ids=true, to_apply=%region_1.0 | all-reduce | flops 32 | bytes 256 | tf_op jit(solution)/shard_map/psum | solution.py:31
  36.0 30.8 %all-gather.8.cloned.1.call-done = bf16[2,256,2048]{2,1,0:T(8,128)(2,1)} async-done(((bf16[2,16,2048]{2,1,0:T(8,128)(2,1)}), bf16[2,256,2048]{2,1,0:T(8,128)(2,1)}) %all-gather.8.cloned.1.call-update) | async-done | bytes 2097168 | tf_op jit(solution)/shard_map/all_gather | solution.py:36
  66.9 6.7 fusion.28
  73.5 6.4 fusion.30
  79.9 3.3 fusion.29
  83.2 3.3 fusion.31
  86.5 157.6 %all-reduce.3.cloned.1.call-done = (f32[256,1664]{1,0:T(8,128)}, f32[256,1664]{1,0:T(8,128)}, f32[256,1664]{1,0:T(8,128)}, f32[256,1664]{1,0:T(8,128)}) async-done(((f32[256,1664]{1,0:T(8,128)}, f32[256,1664]{1,0:T(8,128)}, f32[256,1664]{1,0:T(8,128)}, f32[256,1664]{1,0:T(8,128)}), (f32[256,1664]{1,0:T(8,128)}, f32[256,1664]{1,0:T(8,128)}, f32[256,1664]{1,0:T(8,128)}, ...) | async-done | bytes 6815760 | tf_op jit(solution)/shard_map/psum | solution.py:49
  244.1 7.4 %fusion.33 = f32[256,2048]{1,0:T(8,128)} fusion(bf16[1664,2048]{1,0:T(8,128)(2,1)} %param.17, f32[256,1664]{1,0:T(8,128)} %get-tuple-element.11, f32[256,1664]{1,0:T(8,128)} %get-tuple-element.12), kind=kOutput, calls=%fused_computation.47 | convolution fusion | flops 1747386368 | bytes 12320768 | tf_op jit(solution)/shard_map/dot_general | solution.py:59
  253.0 7.0 fusion.32
  260.1 52.6 %reduce-scatter.5.cloned.1.call-done = f32[16,2048]{1,0:T(8,128)} async-done(((f32[256,2048]{1,0:T(8,128)}), f32[16,2048]{1,0:T(8,128)}) %reduce-scatter.5.cloned.1.call-update) | async-done | bytes 131088 | tf_op jit(solution)/shard_map/reduce_scatter | solution.py:61
  312.7 64.8 %reduce-scatter.3.cloned.1.call-done = f32[16,2048]{1,0:T(8,128)} async-done(((f32[256,2048]{1,0:T(8,128)}), f32[16,2048]{1,0:T(8,128)}) %reduce-scatter.3.cloned.1.call-update) | async-done | bytes 131088 | tf_op jit(solution)/shard_map/reduce_scatter | solution.py:61
  380.0 3.1 copy.28
  384.6 26.3 %all-gather.10.cloned.1.call-done = bf16[256,2048]{1,0:T(8,128)(2,1)} async-done(((bf16[16,2048]{1,0:T(8,128)(2,1)}), bf16[256,2048]{1,0:T(8,128)(2,1)}) %all-gather.10.cloned.1.call-update) | async-done | bytes 1048592 | tf_op jit(solution)/shard_map/all_gather | solution.py:69
  410.9 4.7 gather_fusion.1
  415.6 3.2 fusion.24
  418.9 26.1 %all-gather.12.cloned.1.call-done = bf16[256,2048]{1,0:T(8,128)(2,1)} async-done(((bf16[16,2048]{1,0:T(8,128)(2,1)}), bf16[256,2048]{1,0:T(8,128)(2,1)}) %all-gather.12.cloned.1.call-update) | async-done | bytes 1048592 | tf_op jit(solution)/shard_map/all_gather | solution.py:69
  445.0 4.7 gather_fusion.2
  449.8 3.2 fusion.22
  453.9 83.2 %all-gather.14.cloned.1.call-done = f32[2048,768]{1,0:T(8,128)} async-done(((f32[256,768]{1,0:T(8,128)}), f32[2048,768]{1,0:T(8,128)}) %all-gather.14.cloned.1.call-update) | async-done | bytes 6291472 | tf_op jit(solution)/shard_map/all_gather | solution.py:72
  537.1 3.2 reduce_sum.46
  540.3 86.6 %all-gather.16.cloned.1.call-done = f32[2048,768]{1,0:T(8,128)} async-done(((f32[256,768]{1,0:T(8,128)}), f32[2048,768]{1,0:T(8,128)}) %all-gather.16.cloned.1.call-update) | async-done | bytes 6291472 | tf_op jit(solution)/shard_map/all_gather | solution.py:72
  626.9 3.3 reduce_sum.48
  642.0 54.6 %psum.47 = f32[2,32,14]{1,2,0:T(8,128)S(1)} all-reduce(f32[2,32,14]{1,2,0:T(8,128)S(1)} %pad_maximum_fusion.5), channel_id=1, replica_groups=mesh['tx'=8,'ty'=16] {'ty'}, use_global_device_ids=true, to_apply=%region_15.17 | all-reduce | flops 896 | bytes 7168 | tf_op jit(solution)/shard_map/psum | solution.py:98
  696.7 34.4 %all_gather.31 = f32[2,256,14]{2,0,1:T(2,128)S(1)} all-gather(f32[2,32,14]{2,0,1:T(2,128)S(1)} %copy.33), channel_id=1, replica_groups=mesh['tx'=8,'ty'=16] {'tx'}, dimensions={1}, use_global_device_ids=true | all-gather | bytes 32256 | tf_op jit(solution)/shard_map/all_gather | solution.py:99
  (89 shorter events, 23.8 us)
Async XLA Ops:
  7.2 634.6 %copy-start = (bf16[256,14]{0,1:T(8,128)(2,1)S(1)}, bf16[256,14]{0,1:T(8,128)(2,1)}, u32[]{:S(2)}) copy-start(bf16[256,14]{0,1:T(8,128)(2,1)} %param.19) | copy-start | bytes 21508
  7.2 59.7 %all-gather.8.cloned.1.call-start = ((), (), s32[]{:S(2)}) async-start(), calls=%async_computation.2 | async-start | bytes 2228224 | tf_op jit(solution)/shard_map/all_gather | solution.py:36
  36.0 208.1 %all-reduce.3.cloned.1.call-start = ((), (), s32[]{:S(2)}) async-start(), calls=%async_computation.9 | async-start | bytes 13631488 | tf_op jit(solution)/shard_map/psum | solution.py:49
  66.9 6.7 copy-start.11
  73.5 6.4 copy-start.10
  86.5 226.2 %reduce-scatter.5.cloned.1.call-start = ((), (), s32[]{:S(2)}) async-start(), calls=%async_computation.4 | async-start | bytes 2228224 | tf_op jit(solution)/shard_map/reduce_scatter | solution.py:61
  251.5 1.5 copy-start.12
  251.5 125.9 %reduce-scatter.3.cloned.1.call-start = ((), (), s32[]{:S(2)}) async-start(), calls=%async_computation.3 | async-start | bytes 2228224 | tf_op jit(solution)/shard_map/reduce_scatter | solution.py:61
  253.0 7.0 copy-start.5
  259.9 120.1 %copy-start.3 = (bf16[2048,3,256]{2,0,1:T(8,128)(2,1)S(1)}, bf16[2048,3,256]{2,0,1:T(8,128)(2,1)}, u32[]{:S(2)}) copy-start(bf16[2048,3,256]{2,0,1:T(8,128)(2,1)} %param.18) | copy-start | bytes 9437188
  260.0 150.9 %all-gather.10.cloned.1.call-start = ((), (), s32[]{:S(2)}) async-start(), calls=%async_computation.5 | async-start | bytes 1114112 | tf_op jit(solution)/shard_map/all_gather | solution.py:69
  379.2 65.8 %all-gather.12.cloned.1.call-start = ((), (), s32[]{:S(2)}) async-start(), calls=%async_computation.6 | async-start | bytes 1114112 | tf_op jit(solution)/shard_map/all_gather | solution.py:69
  379.8 3.4 copy-start.9
  379.8 157.3 %all-gather.14.cloned.1.call-start = ((), (), s32[]{:S(2)}) async-start(), calls=%async_computation.7 | async-start | bytes 7077888 | tf_op jit(solution)/shard_map/all_gather | solution.py:72
  384.6 31.0 %copy-start.4 = (bf16[2048,3,256]{0,2,1:T(8,128)(2,1)S(1)}, bf16[2048,3,256]{0,2,1:T(8,128)(2,1)}, u32[]{:S(2)}) copy-start(bf16[2048,3,256]{0,2,1:T(8,128)(2,1)} %copy.28) | copy-start | bytes 9437188
  418.9 208.0 %all-gather.16.cloned.1.call-start = ((), (), s32[]{:S(2)}) async-start(), calls=%async_computation.8 | async-start | bytes 7077888 | tf_op jit(solution)/shard_map/all_gather | solution.py:72
  449.7 3.3 copy-start.8
  449.7 3.4 copy-start.6
  449.7 3.4 copy-start.7
  626.9 3.4 copy-start.1
  630.4 3.3 copy-start.2
Sparse Core Ops, SparseCore 0:
  36.1 30.7 all-gather.7
  86.6 157.4 all-reduce.2
  251.7 60.9 reduce-scatter.4
  314.9 62.5 reduce-scatter.2
  379.6 31.2 all-gather.9
  412.5 32.4 all-gather.11
  447.3 89.7 all-gather.13
  539.4 87.4 all-gather.15
